TPU v7x, 128 devices: a whole 4x4x4 slice. The times are simulated.
128 devices in a mesh: orient: 32 (over x, z, y_lo), slab: 4 (over y_hi, core).
Axes of the slice: x: 4, y: 4 (y_hi: 2, y_lo: 2; y = y_hi * 2 + y_lo), z: 4, core: 2. Of those that a mesh axis runs over, the one named last changes fastest.
Arguments:
- volume: bfloat16 [32, 512, 8192], P('orient', 'slab'), may hold values from 0 to 2
- rays: bfloat16 [8192, 8, 128], replicated, may hold values from -0.0234375 to 0.0234375
- band_start: int32 [8, 32], P(None, 'orient'), may hold values from 0 to 63
- band_len: int32 [8, 32], P(None, 'orient'), may hold values from 32 to 64
- slot_image: int32 [32], replicated, may hold values from 0 to 31, each once
- measured: float32 [32, 512, 128], P('orient', 'slab'), may hold values from -6 to 6
- relax: float32 [32], P('orient'), may hold values from 0.25 to 1
Outputs:
- updated: bfloat16 [32, 512, 8192], P('orient', 'slab')
- residual: float32 [32, 512, 128], P('orient', 'slab')
Inputs may be any that keep to these rules, and one draw needn't show every extreme that they name: `slot_image`: every image number appears in exactly one slot. band_start + band_len stays below 128.
All inputs are finite; a program needn't handle non-finite values.
Results may differ from a plain program's by a relative error of at most 0.0055.
Values may be sent and summed in bfloat16 or wider, within the bound.
No kernel may reach another device: no remote copies, remote signals or barrier semaphores. Data moves between devices by JAX's collectives and lax.ppermute only.
A program may use at most 128 MiB of HBM per device.

v0:
```python
import math
import jax
import jax.numpy as jnp
from jax import lax
from jax.sharding import PartitionSpec as P

FRAMES = 4
SWEEPS = 2
huber_delta = 0.5
sweep_rate = 0.2


def extended_2(cells, sides, width):
    for axis, dim in sides:
        count = lax.axis_size(axis)
        ends = count - 1
        head = lax.slice_in_dim(cells, 0, width, axis=dim)
        tail = lax.slice_in_dim(cells, cells.shape[dim] - width, cells.shape[dim], axis=dim)
        cells = jnp.concatenate(
            [
                lax.ppermute(tail, axis, [(i, (i + 1) % count) for i in range(ends)]),
                cells,
                lax.ppermute(head, axis, [((i + 1) % count, i) for i in range(ends)]),
            ],
            axis=dim,
        )
    return cells


def smooth_pass(extended, first_row, total_rows):
    middle = extended[:, 1:-1]
    row_count = middle.shape[1]
    global_rows = first_row + 1 + jnp.arange(row_count, dtype=jnp.int32)
    has_above = (global_rows > 0)[None, :, None]
    has_below = (global_rows < total_rows - 1)[None, :, None]
    from_above = jnp.clip(middle - extended[:, :-2], -huber_delta, huber_delta)
    from_below = jnp.clip(middle - extended[:, 2:], -huber_delta, huber_delta)
    row_flux = jnp.where(has_above, from_above, 0.0) + jnp.where(has_below, from_below, 0.0)
    return middle - sweep_rate * row_flux


def local(volume, rays, band_start, band_len, slot_image, measured, relax):
    or_dev, row_dev, cell_count = volume.shape
    reflections_n, detector = (rays.shape[1], rays.shape[2])
    images_n = reflections_n * FRAMES
    orient_groups = lax.axis_size("orient")
    orients_all = or_dev * orient_groups
    orient_ids = lax.axis_index("orient") * or_dev + jnp.arange(or_dev, dtype=jnp.int32)
    reflections = jnp.arange(reflections_n, dtype=jnp.int32)
    frame_of = (orient_ids[:, None] + reflections[None, :]) % FRAMES
    frame_pick = (frame_of[:, :, None] == jnp.arange(FRAMES, dtype=jnp.int32)).astype(jnp.float32)
    columns = jnp.arange(detector, dtype=jnp.int32)
    inside = (columns >= band_start[:, :, None]) & (columns < (band_start + band_len)[:, :, None])
    band_mask = inside.astype(jnp.float32)
    inverse = (
        jnp.zeros((images_n,), jnp.int32).at[slot_image].set(jnp.arange(images_n, dtype=jnp.int32))
    )
    flat_rays = rays.reshape(cell_count, reflections_n * detector)
    projected = jnp.dot(
        volume.reshape(or_dev * row_dev, cell_count), flat_rays, preferred_element_type=jnp.float32
    )
    projected = projected.reshape(or_dev, row_dev, reflections_n, detector)
    evolved = jnp.einsum("okf,kod,orkd->kfrd", frame_pick, band_mask, projected)
    ordered = evolved.reshape(images_n, row_dev, detector)[slot_image]
    owned = lax.psum_scatter(ordered, "orient", scatter_dimension=0, tiled=True)
    residual = measured - owned
    everyone = lax.all_gather(residual.astype(jnp.bfloat16), "orient", axis=0, tiled=True)
    by_image = everyone[inverse].reshape(reflections_n, FRAMES, row_dev, detector)
    picked = by_image[reflections[None, :], frame_of]
    masked = picked * jnp.transpose(band_mask, (1, 0, 2))[:, :, None, :].astype(jnp.bfloat16)
    gradient = jnp.einsum("okrd,ckd->orc", masked, rays, preferred_element_type=jnp.float32)
    step_gain = math.sqrt(cell_count * orients_all / (FRAMES * reflections_n * detector))
    density = volume.astype(jnp.float32) + relax[:, None, None] * step_gain * gradient
    total_rows = row_dev * lax.axis_size("slab")
    base_row = lax.axis_index("slab") * row_dev
    for repeat in range(SWEEPS):
        extended = extended_2(density, (("slab", 1),), 1)
        density = smooth_pass(extended, base_row - 1, total_rows)
    return (density.astype(jnp.bfloat16), residual)


def solution(mesh):
    placed = (
        P("orient", "slab", None),
        P(),
        P(None, "orient"),
        P(None, "orient"),
        P(),
        P("orient", "slab", None),
        P("orient"),
    )
    return jax.shard_map(
        local,
        mesh=mesh,
        in_specs=placed,
        out_specs=(P("orient", "slab", None), P("orient", "slab", None)),
        check_vma=False,
    )
```

profile of v0, /device:TPU:1, one launch (start us, length us, event | category | flops | bytes accessed | tf_op | source)
XLA Modules:
  0.0 423.8 jit_solution(1588492112718736785)
XLA Ops:
  7.2 0.0 reduce-scatter.2.cloned.1.call-start
  7.2 15.6 %copy.30 = bf16[1024,8,8,128]{3,1,2,0:T(8,128)(2,1)} copy(bf16[1024,8,8,128]{3,2,1,0:T(8,128)(2,1)} %bitcast.48) | data formatting | bytes 33554432
  22.8 21.1 %copy.15 = bf16[1024,8192]{1,0:T(8,128)(2,1)} copy(bf16[1024,8192]{0,1:T(8,128)(2,1)} %bitcast.47) | data formatting | bytes 33554432 | tf_op jit(solution)/shard_map/dot_general | solution.py:59
  43.9 0.1 fusion.46
  44.0 0.0 copy-done.2
  44.0 8.1 %fusion.38 = f32[8,128,128]{1,2,0:T(8,128)S(1)} fusion(bf16[8,128,8192]{2,1,0:T(8,128)(2,1)} %bitcast.49, bf16[1,128,8192]{2,1,0:T(8,128)(2,1)S(1)} %copy-done.2, f32[8,128]{1,0:T(8,128)S(1)} %get-tuple-element.9), kind=kOutput, calls=%fused_computation.37 | convolution fusion | flops 2147614720 | bytes 19402752 | tf_op jit(solution)/shard_map/dot_general | solution.py:59
  52.2 0.2 copy.16
  52.4 0.1 fusion.43
  52.5 0.0 copy-start
  52.5 0.2 broadcast_multiply_fusion
  52.7 2.0 gather_fusion
  54.7 0.0 reduce-scatter.2.cloned.1.call-update
  54.7 0.0 all-gather.2.cloned.1.call-start
  54.8 144.4 %reduce-scatter.2.cloned.1.call-done = f32[1,128,128]{2,1,0:T(8,128)} async-done(((f32[32,128,128]{2,1,0:T(8,128)}), f32[1,128,128]{2,1,0:T(8,128)}) %reduce-scatter.2.cloned.1.call-update) | async-done | bytes 65552 | tf_op jit(solution)/shard_map/reduce_scatter | solution.py:65
  199.1 1.5 fusion.53
  200.6 0.0 all-gather.2.cloned.1.call-update
  201.3 0.7 scatter_custom_fusion
  202.1 147.3 %all-gather.2.cloned.1.call-done = bf16[32,128,128]{2,1,0:T(8,128)(2,1)} async-done(((bf16[1,128,128]{2,1,0:T(8,128)(2,1)}), bf16[32,128,128]{2,1,0:T(8,128)(2,1)}) %all-gather.2.cloned.1.call-update) | async-done | bytes 1048592 | tf_op jit(solution)/shard_map/all_gather | solution.py:67
  349.3 2.0 gather_fusion.1
  351.3 0.6 gather_fusion.2
  351.9 14.0 %fusion.11 = f32[1,128,8192]{2,1,0:T(8,128)} fusion(bf16[8192,8,128]{2,1,0:T(8,128)(2,1)} %param.8, bf16[1,128,8192]{2,1,0:T(8,128)(2,1)} %param.7, f32[]{:T(128)} %bitcast, bf16[8,128,128]{2,1,0:T(8,128)(2,1)S(1)} %gather_fusion.2, bf16[8,128]{1,0:T(8,128)(2,1)S(1)} %get-tuple-element.8), kind=kOutput, calls=%fused_computation.10 | convolution fusion | flops 2150760448 | bytes 23332868 | tf_op jit(solution)/shard_map/okrd,ckd->orc/dot_general | solution.py:71
  365.9 1.1 fusion.55
  367.0 25.5 %collective-permute-start.1 = (f32[1,1,8192]{2,1,0:T(1,128)S(1)}, f32[1,1,8192]{2,1,0:T(1,128)S(1)}, u32[]{:S(2)}, u32[]{:S(2)}) collective-permute-start(f32[1,1,8192]{2,1,0:T(1,128)S(1)} %get-tuple-element.7), channel_id=1, source_target_pairs={{1,0},{2,1},{3,2},{5,4},{6,5},{7,6},{9,8},{10,9},{11,10},{13,12},{... | collective-permute-start | bytes 98312 | tf_op jit(solution)/shard_map/ppermute | solution.py:23
  392.5 4.6 %collective-permute-start = (f32[1,1,8192]{2,1,0:T(1,128)S(1)}, f32[1,1,8192]{2,1,0:T(1,128)S(1)}, u32[]{:S(2)}, u32[]{:S(2)}) collective-permute-start(f32[1,1,8192]{2,1,0:T(1,128)S(1)} %get-tuple-element.6), channel_id=1, source_target_pairs={{0,1},{1,2},{2,3},{4,5},{5,6},{6,7},{8,9},{9,10},{10,11},{12,13},{... | collective-permute-start | bytes 98312 | tf_op jit(solution)/shard_map/ppermute | solution.py:21
  397.1 0.0 collective-permute-done.1
  397.1 1.0 collective-permute-done
  398.1 6.0 %fusion.29 = f32[1,128,8192]{2,1,0:T(8,128)S(1)} fusion(f32[1,128,8192]{2,1,0:T(8,128)} %fusion.11, f32[1,1,8192]{2,1,0:T(1,128)S(1)} %collective-permute-done.1, f32[1,1,8192]{2,1,0:T(1,128)S(1)} %collective-permute-done, pred[128]{0:T(512)(128)(4,1)S(1)} %get-tuple-element.10, pred[128]{0:T(512)(128)(4,1)S(1)} %get-tuple-element.11), kind=kLoop, calls=%fused_computation.29 | loop fusion | flops 11534336 | bytes 8454400 | tf_op jit(solution)/shard_map/sub | solution.py:39
  404.1 1.9 collective-permute-start.3
  406.1 5.7 %collective-permute-start.2 = (f32[1,1,8192]{2,1,0:T(1,128)S(1)}, f32[1,1,8192]{2,1,0:T(1,128)S(1)}, u32[]{:S(2)}, u32[]{:S(2)}) collective-permute-start(f32[1,1,8192]{2,1,0:T(1,128)S(1)} %get-tuple-element.4), channel_id=1, source_target_pairs={{0,1},{1,2},{2,3},{4,5},{5,6},{6,7},{8,9},{9,10},{10,11},{12,13},{... | collective-permute-start | bytes 98312 | tf_op jit(solution)/shard_map/ppermute | solution.py:21
  411.8 0.0 collective-permute-done.3
  411.8 1.0 collective-permute-done.2
  412.8 4.2 fusion.20
  (21 shorter events, 0.1 us)
Async XLA Ops:
  7.2 192.0 %reduce-scatter.2.cloned.1.call-start = ((), (), s32[]{:S(2)}) async-start(), calls=%async_computation.1 | async-start | bytes 2162688 | tf_op jit(solution)/shard_map/reduce_scatter | solution.py:65
  22.8 21.1 %copy-start.1 = (s32[8,1]{0,1:T(1,128)S(1)}, s32[8,1]{0,1:T(1,128)}, u32[]{:S(2)}) copy-start(s32[8,1]{0,1:T(1,128)} %param.9) | copy-start | bytes 100
  22.8 21.1 %copy-start.3 = (s32[8,1]{0,1:T(1,128)S(1)}, s32[8,1]{0,1:T(1,128)}, u32[]{:S(2)}) copy-start(s32[8,1]{0,1:T(1,128)} %param.10) | copy-start | bytes 100
  22.8 21.2 %copy-start.2 = (bf16[1,128,8192]{2,1,0:T(8,128)(2,1)S(1)}, bf16[1,128,8192]{2,1,0:T(8,128)(2,1)}, u32[]{:S(2)}) copy-start(bf16[1,128,8192]{2,1,0:T(8,128)(2,1)} %param.7) | copy-start | bytes 6291460
  44.0 8.4 %copy-start.4 = (s32[32]{0:T(128)S(1)}, s32[32]{0:T(128)}, u32[]{:S(2)}) copy-start(s32[32]{0:T(128)} %param.11) | copy-start | bytes 388
  52.5 146.7 %copy-start = (f32[1,128,128]{2,1,0:T(8,128)S(1)}, f32[1,128,128]{2,1,0:T(8,128)}, u32[]{:S(2)}) copy-start(f32[1,128,128]{2,1,0:T(8,128)} %param.12) | copy-start | bytes 196612
  54.7 294.6 %all-gather.2.cloned.1.call-start = ((), (), s32[]{:S(2)}) async-start(), calls=%async_computation.2 | async-start | bytes 1081344 | tf_op jit(solution)/shard_map/all_gather | solution.py:67
  367.0 30.1 %collective-permute-start.1 = (f32[1,1,8192]{2,1,0:T(1,128)S(1)}, f32[1,1,8192]{2,1,0:T(1,128)S(1)}, u32[]{:S(2)}, u32[]{:S(2)}) collective-permute-start(f32[1,1,8192]{2,1,0:T(1,128)S(1)} %get-tuple-element.7), channel_id=1, source_target_pairs={{1,0},{2,1},{3,2},{5,4},{6,5},{7,6},{9,8},{10,9},{11,10},{13,12},{... | collective-permute-start | bytes 98312 | tf_op jit(solution)/shard_map/ppermute | solution.py:23
  392.5 5.6 %collective-permute-start = (f32[1,1,8192]{2,1,0:T(1,128)S(1)}, f32[1,1,8192]{2,1,0:T(1,128)S(1)}, u32[]{:S(2)}, u32[]{:S(2)}) collective-permute-start(f32[1,1,8192]{2,1,0:T(1,128)S(1)} %get-tuple-element.6), channel_id=1, source_target_pairs={{0,1},{1,2},{2,3},{4,5},{5,6},{6,7},{8,9},{9,10},{10,11},{12,13},{... | collective-permute-start | bytes 98312 | tf_op jit(solution)/shard_map/ppermute | solution.py:21
  404.1 7.7 %collective-permute-start.3 = (f32[1,1,8192]{2,1,0:T(1,128)S(1)}, f32[1,1,8192]{2,1,0:T(1,128)S(1)}, u32[]{:S(2)}, u32[]{:S(2)}) collective-permute-start(f32[1,1,8192]{2,1,0:T(1,128)S(1)} %get-tuple-element.5), channel_id=1, source_target_pairs={{1,0},{2,1},{3,2},{5,4},{6,5},{7,6},{9,8},{10,9},{11,10},{13,12},{... | collective-permute-start | bytes 98312 | tf_op jit(solution)/shard_map/ppermute | solution.py:23
  406.1 6.7 %collective-permute-start.2 = (f32[1,1,8192]{2,1,0:T(1,128)S(1)}, f32[1,1,8192]{2,1,0:T(1,128)S(1)}, u32[]{:S(2)}, u32[]{:S(2)}) collective-permute-start(f32[1,1,8192]{2,1,0:T(1,128)S(1)} %get-tuple-element.4), channel_id=1, source_target_pairs={{0,1},{1,2},{2,3},{4,5},{5,6},{6,7},{8,9},{9,10},{10,11},{12,13},{... | collective-permute-start | bytes 98312 | tf_op jit(solution)/shard_map/ppermute | solution.py:21
Sparse Core Ops, SparseCore 0:
  54.9 144.2 reduce-scatter.1
  201.3 147.9 all-gather.1
where the time goes:
time: 425 us; the launch traced here: 424 us
  waiting for transfers between devices  294 us (69%)
  local copies, waits for them, and re-layouts  43.3 us (10%)
  starting transfers between devices  37.8 us (9%)
  matrix products  22.1 us (5%)
  between operations  14.9 us (4%)
  other arithmetic  12.1 us (3%)
    all_gather x1, waiting for transfers between devices, local(): lax.all_gather(residual.astype(jnp.bfloat16), 'orient', axis=0, tiled=True)  147 us
    reduce_scatter x1, waiting for transfers between devices, local(): owned = lax.psum_scatter(ordered, 'orient', scatter_dimension=0, tiled=True)  144 us
    ppermute x2, starting transfers between devices, extended_2(): lax.ppermute(head, axis, [((i + 1) % count, i) for i in range(ends)])  27.4 us
    dot_general x1, local copies, waits for them, and re-layouts, local(): jnp.dot(volume.reshape(or_dev * row_dev, cell_count), flat_rays, preferre...  21.1 us
    unnamed x11, local copies, waits for them, and re-layouts  15.6 us
    dot_general x1, matrix products, local(): jnp.einsum('okrd,ckd->orc', masked, rays, preferred_element_type=jnp.floa...  14 us
    ppermute x2, starting transfers between devices, extended_2(): lax.ppermute(tail, axis, [(i, (i + 1) % count) for i in range(ends)])  10.3 us
  transfers between devices with their start and end apart: 6, of which 4 were waited for; matrix products, arithmetic and copies ran while one was open for 0% of the time, Pallas kernels for 0%

commit v1 on v0

--- a/solution.py
+++ b/solution.py
@@ -64,7 +64,12 @@
     ordered = evolved.reshape(images_n, row_dev, detector)[slot_image]
     owned = lax.psum_scatter(ordered, "orient", scatter_dimension=0, tiled=True)
     residual = measured - owned
-    everyone = lax.all_gather(residual.astype(jnp.bfloat16), "orient", axis=0, tiled=True)
+    everyone = jnp.concatenate(
+        lax.all_to_all(
+            jnp.stack(lax.axis_size("orient") * [residual.astype(jnp.bfloat16)]), "orient", 0, 0
+        ),
+        0,
+    )
     by_image = everyone[inverse].reshape(reflections_n, FRAMES, row_dev, detector)
     picked = by_image[reflections[None, :], frame_of]
     masked = picked * jnp.transpose(band_mask, (1, 0, 2))[:, :, None, :].astype(jnp.bfloat16)

time: 425 us -> 295 us (0.69)
  waiting for transfers between devices: 294 us -> 158 us
  starting transfers between devices: 37.8 us -> 43.5 us
    all_gather x1 -> x0, waiting for transfers between devices: 147 us -> none  [local(): lax.all_gather(residual.astype(jnp.bfloat16), 'orient', axis=0, tiled=True)]
    all_to_all x0 -> x1, waiting for transfers between devices: none -> 10.7 us  [local(): lax.all_to_all(jnp.stack(lax.axis_size('orient') * [residual.astype(jnp.b...]
where the time goes in v1:
time: 295 us; the launch traced here: 294 us
  waiting for transfers between devices  158 us (54%)
  local copies, waits for them, and re-layouts  43.7 us (15%)
  starting transfers between devices  43.5 us (15%)
  matrix products  22.1 us (7%)
  between operations  14.9 us (5%)
  other arithmetic  12.3 us (4%)
    reduce_scatter x1, waiting for transfers between devices, local(): owned = lax.psum_scatter(ordered, 'orient', scatter_dimension=0, tiled=True)  145 us
    ppermute x2, starting transfers between devices, extended_2(): lax.ppermute(head, axis, [((i + 1) % count, i) for i in range(ends)])  29.8 us
    dot_general x1, local copies, waits for them, and re-layouts, local(): jnp.dot(volume.reshape(or_dev * row_dev, cell_count), flat_rays, preferre...  21.5 us
    unnamed x11, local copies, waits for them, and re-layouts  15.6 us
    dot_general x1, matrix products, local(): jnp.einsum('okrd,ckd->orc', masked, rays, preferred_element_type=jnp.floa...  14 us
    all_to_all x1, waiting for transfers between devices, local(): lax.all_to_all(jnp.stack(lax.axis_size('orient') * [residual.astype(jnp.b...  10.7 us
    ppermute x2, starting transfers between devices, extended_2(): lax.ppermute(tail, axis, [(i, (i + 1) % count) for i in range(ends)])  9.73 us
    dot_general x1, matrix products, local(): jnp.dot(volume.reshape(or_dev * row_dev, cell_count), flat_rays, preferre...  8.14 us
  transfers between devices with their start and end apart: 6, of which 4 were waited for; matrix products, arithmetic and copies ran while one was open for 0% of the time, Pallas kernels for 0%

profile of v1, /device:TPU:1, one launch (start us, length us, event | category | flops | bytes accessed | tf_op | source)
XLA Modules:
  0.0 294.2 jit_solution(17373795660445218193)
XLA Ops:
  7.2 0.0 reduce-scatter.2.cloned.1.call-start
  7.2 15.6 %copy.27 = bf16[1024,8,8,128]{3,1,2,0:T(8,128)(2,1)} copy(bf16[1024,8,8,128]{3,2,1,0:T(8,128)(2,1)} %bitcast.51) | data formatting | bytes 33554432
  22.8 21.5 %copy.12 = bf16[1024,8192]{1,0:T(8,128)(2,1)} copy(bf16[1024,8192]{0,1:T(8,128)(2,1)} %bitcast.50) | data formatting | bytes 33554432 | tf_op jit(solution)/shard_map/dot_general | solution.py:59
  44.3 0.0 copy-done.1
  44.3 0.1 fusion.46
  44.4 8.1 %fusion.38 = f32[8,128,128]{1,2,0:T(8,128)S(1)} fusion(bf16[8,128,8192]{2,1,0:T(8,128)(2,1)} %bitcast.52, bf16[1,128,8192]{2,1,0:T(8,128)(2,1)S(1)} %copy-done.2, f32[8,128]{1,0:T(8,128)S(1)} %get-tuple-element.9), kind=kOutput, calls=%fused_computation.37 | convolution fusion | flops 2147614720 | bytes 19402752 | tf_op jit(solution)/shard_map/dot_general | solution.py:59
  52.5 0.2 copy.13
  52.8 0.1 fusion.43
  52.8 0.0 copy-start
  52.9 0.2 broadcast_multiply_fusion
  53.1 2.0 gather_fusion
  55.1 0.0 reduce-scatter.2.cloned.1.call-update
  55.1 145.1 %reduce-scatter.2.cloned.1.call-done = f32[1,128,128]{2,1,0:T(8,128)} async-done(((f32[32,128,128]{2,1,0:T(8,128)}), f32[1,128,128]{2,1,0:T(8,128)}) %reduce-scatter.2.cloned.1.call-update) | async-done | bytes 65552 | tf_op jit(solution)/shard_map/reduce_scatter | solution.py:65
  200.2 1.5 convert_bitcast_fusion
  201.7 1.2 stack.2
  202.9 3.9 %all-to-all-start = ((bf16[32,1,128,128]{3,2,1,0:T(8,128)(2,1)}), bf16[32,1,128,128]{3,2,1,0:T(8,128)(2,1)S(1)}, u32[]{:S(2)}, u32[]{:S(2)}) async-start(bf16[32,1,128,128]{3,2,1,0:T(8,128)(2,1)} %stack.2), calls=%async_computation.1 | async-start | bytes 2097152 | tf_op jit(solution)/shard_map/all_to_all | solution.py:68
  207.5 0.7 scatter_custom_fusion
  208.2 10.7 %all-to-all-done = bf16[32,1,128,128]{3,2,1,0:T(8,128)(2,1)S(1)} async-done(((bf16[32,1,128,128]{3,2,1,0:T(8,128)(2,1)}), bf16[32,1,128,128]{3,2,1,0:T(8,128)(2,1)S(1)}, u32[]{:S(2)}, u32[]{:S(2)}) %all-to-all-start) | async-done | bytes 1048608 | tf_op jit(solution)/shard_map/all_to_all | solution.py:68
  218.9 0.7 gather_fusion.1
  219.7 0.6 gather_fusion.2
  220.3 14.0 %fusion.11 = f32[1,128,8192]{2,1,0:T(8,128)} fusion(bf16[8192,8,128]{2,1,0:T(8,128)(2,1)} %param.8, bf16[1,128,8192]{2,1,0:T(8,128)(2,1)} %param.7, f32[]{:T(128)} %bitcast, bf16[8,128,128]{2,1,0:T(8,128)(2,1)S(1)} %gather_fusion.2, bf16[8,128]{1,0:T(8,128)(2,1)S(1)} %get-tuple-element.8), kind=kOutput, calls=%fused_computation.10 | convolution fusion | flops 2150760448 | bytes 23332868 | tf_op jit(solution)/shard_map/okrd,ckd->orc/dot_general | solution.py:76
  234.3 1.1 fusion.54
  235.4 27.9 %collective-permute-start.1 = (f32[1,1,8192]{2,1,0:T(1,128)S(1)}, f32[1,1,8192]{2,1,0:T(1,128)S(1)}, u32[]{:S(2)}, u32[]{:S(2)}) collective-permute-start(f32[1,1,8192]{2,1,0:T(1,128)S(1)} %get-tuple-element.7), channel_id=1, source_target_pairs={{1,0},{2,1},{3,2},{5,4},{6,5},{7,6},{9,8},{10,9},{11,10},{13,12},{... | collective-permute-start | bytes 98312 | tf_op jit(solution)/shard_map/ppermute | solution.py:23
  263.2 4.0 %collective-permute-start = (f32[1,1,8192]{2,1,0:T(1,128)S(1)}, f32[1,1,8192]{2,1,0:T(1,128)S(1)}, u32[]{:S(2)}, u32[]{:S(2)}) collective-permute-start(f32[1,1,8192]{2,1,0:T(1,128)S(1)} %get-tuple-element.6), channel_id=1, source_target_pairs={{0,1},{1,2},{2,3},{4,5},{5,6},{6,7},{8,9},{9,10},{10,11},{12,13},{... | collective-permute-start | bytes 98312 | tf_op jit(solution)/shard_map/ppermute | solution.py:21
  267.3 0.0 collective-permute-done.1
  267.3 1.0 collective-permute-done
  268.3 6.2 %fusion.29 = f32[1,128,8192]{2,1,0:T(8,128)S(1)} fusion(f32[1,128,8192]{2,1,0:T(8,128)} %fusion.11, f32[1,1,8192]{2,1,0:T(1,128)S(1)} %collective-permute-done.1, f32[1,1,8192]{2,1,0:T(1,128)S(1)} %collective-permute-done, pred[128]{0:T(512)(128)(4,1)S(1)} %get-tuple-element.10, pred[128]{0:T(512)(128)(4,1)S(1)} %get-tuple-element.11), kind=kLoop, calls=%fused_computation.29 | loop fusion | flops 11534336 | bytes 8454400 | tf_op jit(solution)/shard_map/sub | solution.py:39
  274.5 1.9 collective-permute-start.3
  276.5 5.7 %collective-permute-start.2 = (f32[1,1,8192]{2,1,0:T(1,128)S(1)}, f32[1,1,8192]{2,1,0:T(1,128)S(1)}, u32[]{:S(2)}, u32[]{:S(2)}) collective-permute-start(f32[1,1,8192]{2,1,0:T(1,128)S(1)} %get-tuple-element.4), channel_id=1, source_target_pairs={{0,1},{1,2},{2,3},{4,5},{5,6},{6,7},{8,9},{9,10},{10,11},{12,13},{... | collective-permute-start | bytes 98312 | tf_op jit(solution)/shard_map/ppermute | solution.py:21
  282.2 0.0 collective-permute-done.3
  282.2 1.0 collective-permute-done.2
  283.2 4.2 %fusion.20 = bf16[1,128,8192]{2,1,0:T(8,128)(2,1)} fusion(f32[1,128,8192]{2,1,0:T(8,128)S(1)} %fusion.29, f32[1,1,8192]{2,1,0:T(1,128)S(1)} %collective-permute-done.3, f32[1,1,8192]{2,1,0:T(1,128)S(1)} %collective-permute-done.2, pred[128]{0:T(512)(128)(4,1)S(1)} %get-tuple-element.10, pred[128]{0:T(512)(128)(4,1)S(1)} %get-tuple-element.11), kind=kLoop, calls=%fused_computation.18 | loop fusion | flops 12582912 | bytes 6357248 | tf_op jit(solution)/shard_map/convert_element_type | solution.py:84
  (21 shorter events, 0.1 us)
Async XLA Ops:
  7.2 193.0 %reduce-scatter.2.cloned.1.call-start = ((), (), s32[]{:S(2)}) async-start(), calls=%async_computation.2 | async-start | bytes 2162688 | tf_op jit(solution)/shard_map/reduce_scatter | solution.py:65
  22.8 21.5 %copy-start.1 = (s32[8,1]{0,1:T(1,128)S(1)}, s32[8,1]{0,1:T(1,128)}, u32[]{:S(2)}) copy-start(s32[8,1]{0,1:T(1,128)} %param.9) | copy-start | bytes 100
  22.8 21.5 %copy-start.3 = (s32[8,1]{0,1:T(1,128)S(1)}, s32[8,1]{0,1:T(1,128)}, u32[]{:S(2)}) copy-start(s32[8,1]{0,1:T(1,128)} %param.10) | copy-start | bytes 100
  22.8 21.6 %copy-start.2 = (bf16[1,128,8192]{2,1,0:T(8,128)(2,1)S(1)}, bf16[1,128,8192]{2,1,0:T(8,128)(2,1)}, u32[]{:S(2)}) copy-start(bf16[1,128,8192]{2,1,0:T(8,128)(2,1)} %param.7) | copy-start | bytes 6291460
  44.4 8.4 %copy-start.4 = (s32[32]{0:T(128)S(1)}, s32[32]{0:T(128)}, u32[]{:S(2)}) copy-start(s32[32]{0:T(128)} %param.11) | copy-start | bytes 388
  52.8 147.3 %copy-start = (f32[1,128,128]{2,1,0:T(8,128)S(1)}, f32[1,128,128]{2,1,0:T(8,128)}, u32[]{:S(2)}) copy-start(f32[1,128,128]{2,1,0:T(8,128)} %param.12) | copy-start | bytes 196612
  202.9 16.1 %all-to-all-start = ((bf16[32,1,128,128]{3,2,1,0:T(8,128)(2,1)}), bf16[32,1,128,128]{3,2,1,0:T(8,128)(2,1)S(1)}, u32[]{:S(2)}, u32[]{:S(2)}) async-start(bf16[32,1,128,128]{3,2,1,0:T(8,128)(2,1)} %stack.2), calls=%async_computation.1 | async-start | bytes 2097152 | tf_op jit(solution)/shard_map/all_to_all | solution.py:68
  235.4 31.9 %collective-permute-start.1 = (f32[1,1,8192]{2,1,0:T(1,128)S(1)}, f32[1,1,8192]{2,1,0:T(1,128)S(1)}, u32[]{:S(2)}, u32[]{:S(2)}) collective-permute-start(f32[1,1,8192]{2,1,0:T(1,128)S(1)} %get-tuple-element.7), channel_id=1, source_target_pairs={{1,0},{2,1},{3,2},{5,4},{6,5},{7,6},{9,8},{10,9},{11,10},{13,12},{... | collective-permute-start | bytes 98312 | tf_op jit(solution)/shard_map/ppermute | solution.py:23
  263.2 5.0 %collective-permute-start = (f32[1,1,8192]{2,1,0:T(1,128)S(1)}, f32[1,1,8192]{2,1,0:T(1,128)S(1)}, u32[]{:S(2)}, u32[]{:S(2)}) collective-permute-start(f32[1,1,8192]{2,1,0:T(1,128)S(1)} %get-tuple-element.6), channel_id=1, source_target_pairs={{0,1},{1,2},{2,3},{4,5},{5,6},{6,7},{8,9},{9,10},{10,11},{12,13},{... | collective-permute-start | bytes 98312 | tf_op jit(solution)/shard_map/ppermute | solution.py:21
  274.5 7.7 %collective-permute-start.3 = (f32[1,1,8192]{2,1,0:T(1,128)S(1)}, f32[1,1,8192]{2,1,0:T(1,128)S(1)}, u32[]{:S(2)}, u32[]{:S(2)}) collective-permute-start(f32[1,1,8192]{2,1,0:T(1,128)S(1)} %get-tuple-element.5), channel_id=1, source_target_pairs={{1,0},{2,1},{3,2},{5,4},{6,5},{7,6},{9,8},{10,9},{11,10},{13,12},{... | collective-permute-start | bytes 98312 | tf_op jit(solution)/shard_map/ppermute | solution.py:23
  276.5 6.7 %collective-permute-start.2 = (f32[1,1,8192]{2,1,0:T(1,128)S(1)}, f32[1,1,8192]{2,1,0:T(1,128)S(1)}, u32[]{:S(2)}, u32[]{:S(2)}) collective-permute-start(f32[1,1,8192]{2,1,0:T(1,128)S(1)} %get-tuple-element.4), channel_id=1, source_target_pairs={{0,1},{1,2},{2,3},{4,5},{5,6},{6,7},{8,9},{9,10},{10,11},{12,13},{... | collective-permute-start | bytes 98312 | tf_op jit(solution)/shard_map/ppermute | solution.py:21
Sparse Core Ops, SparseCore 0:
  55.2 144.9 reduce-scatter.1
